TPU v7x, 128 devices: a whole 4x4x4 slice. The times are simulated.
128 devices in a mesh: group: 8 (over x, z_hi), space: 16 (over y, z_lo, core).
Axes of the slice: x: 4, y: 4, z: 4 (z_hi: 2, z_lo: 2; z = z_hi * 2 + z_lo), core: 2. Of those that a mesh axis runs over, the one named last changes fastest.
Arguments:
- prev_field: float32 [8, 256, 256, 256], P('group', 'space'), may hold values from -6 to 6
- curr_field: float32 [8, 256, 256, 256], P('group', 'space'), may hold values from -6 to 6
- coefficient: float32 [256, 256, 256], P('space'), may hold values from 0.05 to 0.2
- recordings: float32 [8, 2, 512], P('group'), may hold values from -24 to 24
- receivers: int32 [8, 512], P('group'), may hold values from 0 to 16777215
- image_in: float32 [128, 128, 128], P('space', 'group'), may hold values from -6 to 6
Outputs:
- final_field: float32 [8, 256, 256, 256], P('group', 'space')
- image_out: float32 [128, 128, 128], P('space', 'group')
All inputs are finite; a program needn't handle non-finite values.
Results may differ from a plain program's by a relative error of at most 0.00002.
Values sent between devices are 32-bit elements; how exact they have to be, the bound alone decides.
A program may use at most 128 MiB of HBM per device.

v0:
```python
import jax
import jax.numpy as jnp
from jax import lax
from jax.sharding import PartitionSpec as P

STEPS = 2
DEC = 2


COEF = (-205.0 / 72.0, 8.0 / 5.0, -1.0 / 5.0, 8.0 / 315.0, -1.0 / 560.0)


def with_halo(block, sides, width):
    for axis, dim in sides:
        count = lax.axis_size(axis)
        forward = [(i, i + 1) for i in range(count - 1)]
        backward = [(target, source) for source, target in forward]
        low = lax.ppermute(
            lax.slice_in_dim(block, block.shape[dim] - width, None, axis=dim), axis, forward
        )
        high = lax.ppermute(lax.slice_in_dim(block, 0, width, axis=dim), axis, backward)
        block = jnp.concatenate([low, block, high], axis=dim)
    return block


def laplace(zpadded):
    nz = zpadded.shape[0] - 8
    nx = zpadded.shape[1]
    ny = zpadded.shape[2]
    full = jnp.pad(zpadded, ((0, 0), (4, 4), (4, 4)))
    centre = zpadded[4 : 4 + nz]
    total = 3.0 * COEF[0] * centre
    for j in range(1, 5):
        side = zpadded[4 + j : 4 + j + nz] + zpadded[4 - j : 4 - j + nz]
        side = (
            side
            + full[4 : 4 + nz, 4 + j : 4 + j + nx, 4 : 4 + ny]
            + full[4 : 4 + nz, 4 - j : 4 - j + nx, 4 : 4 + ny]
        )
        side = (
            side
            + full[4 : 4 + nz, 4 : 4 + nx, 4 + j : 4 + j + ny]
            + full[4 : 4 + nz, 4 : 4 + nx, 4 - j : 4 - j + ny]
        )
        total = total + COEF[j] * side
    return total


def inject(nxt, coef_planes, first_plane, record_now, index):
    plane_size = nxt.shape[1] * nxt.shape[2]
    planes = nxt.shape[0]
    zpos = index // plane_size - first_plane
    valid = (zpos >= 0) & (zpos < planes)
    local = jnp.where(valid, zpos * plane_size + index % plane_size, 0)
    amount = jnp.where(valid, coef_planes.reshape(-1)[local] * record_now, 0.0)
    return nxt.reshape(-1).at[local].add(amount).reshape(nxt.shape)


def geo_mean(fields):
    return jnp.exp(jnp.mean(jnp.log(1.0 + fields * fields), axis=0)) - 1.0


def on_device(prev_field, curr_field, coefficient, recordings, receivers, image_in):
    prev = prev_field[0]
    curr = curr_field[0]
    record = recordings[0]
    index = receivers[0]
    depth = curr.shape[0]
    slab = lax.axis_index("space")
    for step in range(STEPS):
        padded = with_halo(curr, (("space", 0),), 4)
        nxt = 2.0 * curr - prev + coefficient * laplace(padded)
        nxt = inject(nxt, coefficient, slab * depth, record[step], index)
        prev, curr = (curr, nxt)
    sample = curr[::DEC, ::DEC, ::DEC]
    update = geo_mean(
        lax.all_to_all(sample[None], "group", split_axis=2, concat_axis=0, tiled=True)
    )
    return (curr[None], image_in + update)


def solution(mesh):
    placed = (
        P("group", "space", None, None),
        P("group", "space", None, None),
        P("space", None, None),
        P("group", None, None),
        P("group", None),
        P("space", "group", None),
    )
    return jax.shard_map(
        on_device,
        mesh=mesh,
        in_specs=placed,
        out_specs=(P("group", "space", None, None), P("space", "group", None)),
        check_vma=False,
    )
```

profile of v0, /device:TPU:1, one launch (start us, length us, event | category | flops | bytes accessed | tf_op | source)
XLA Modules:
  0.0 246.7 jit_solution(16478315855580566975)
XLA Ops:
  0.6 2.7 %slice_bitcast_fusion.1 = (f32[4,256,256]{2,1,0:T(8,128)}, f32[4,256,256]{2,1,0:T(8,128)S(1)}) fusion(f32[1,16,256,256]{3,2,1,0:T(8,128)} %param.7), kind=kLoop, calls=%fused_computation.96 | loop fusion | bytes 4194304 | tf_op jit(solution)/shard_map/slice | solution.py:21
  3.3 3.3 %collective-permute-start = (f32[4,256,256]{2,1,0:T(8,128)}, f32[4,256,256]{2,1,0:T(8,128)S(1)}, u32[]{:S(2)}, u32[]{:S(2)}) collective-permute-start(f32[4,256,256]{2,1,0:T(8,128)} %get-tuple-element.8), channel_id=1, source_target_pairs={{1,0},{2,1},{3,2},{4,3},{5,4},{6,5},{7,6},{8,7},{9,8},{10,9},{11,1... | collective-permute-start | bytes 3145736 | tf_op jit(solution)/shard_map/ppermute | solution.py:21
  6.7 3.5 %collective-permute-start.1 = (f32[4,256,256]{2,1,0:T(8,128)S(1)}, f32[4,256,256]{2,1,0:T(8,128)S(1)}, u32[]{:S(2)}, u32[]{:S(2)}) collective-permute-start(f32[4,256,256]{2,1,0:T(8,128)S(1)} %get-tuple-element.9), channel_id=1, source_target_pairs={{0,1},{1,2},{2,3},{3,4},{4,5},{5,6},{6,7},{7,8},{8,9},{9,10},{10,1... | collective-permute-start | bytes 3145736 | tf_op jit(solution)/shard_map/ppermute | solution.py:18
  10.2 0.0 copy-start.4
  10.2 0.0 copy-start.5
  10.2 6.4 %copy.13 = f32[512,2,8,128]{3,1,2,0:T(2,128)} copy(f32[512,2,8,128]{3,2,1,0:T(8,128)} %bitcast.41) | data formatting | bytes 8388608
  16.6 0.0 copy-done.4
  16.6 20.0 %gather_fusion = f32[512]{0:T(512)S(1)} fusion(f32[1048576]{0:T(1024)} %bitcast.44, s32[1024]{0:T(1024)S(1)} %pad_clamp_fusion), kind=kCustom, calls=%fused_computation | custom fusion | bytes 6144 | tf_op jit(solution)/shard_map/gather | solution.py:55
  36.7 0.0 copy-done.5
  36.7 0.0 collective-permute-done
  36.7 0.0 collective-permute-done.1
  36.7 8.7 %select_maximum_fusion.2 = f32[24,264,264]{2,1,0:T(8,128)} fusion(f32[4,256,256]{2,1,0:T(8,128)S(1)} %collective-permute-done, f32[16,256,256]{2,1,0:T(8,128)} %bitcast.38, f32[4,256,256]{2,1,0:T(8,128)S(1)} %collective-permute-done.1), kind=kLoop, calls=%fused_computation.9 | loop fusion | flops 25090560 | bytes 12982272 | tf_op jit(solution)/shard_map/concatenate | solution.py:22
  45.5 71.2 %fusion.13 = f32[16,256,256]{2,1,0:T(8,128)} fusion(f32[16,256,256]{2,1,0:T(8,128)} %param.8, f32[16,256,256]{2,1,0:T(8,128)} %bitcast.39, f32[4,256,256]{2,1,0:T(8,128)S(1)} %collective-permute-done.1, f32[4,256,256]{2,1,0:T(8,128)S(1)} %collective-permute-done, f32[24,264,264]{2,1,0:T(8,128)} %select_maximum_fusion.2, f32[1,16,256,256]{3,2,1,0:T(8,128)} %param.6), kind=kLoop, calls=%fused_computation.36 | loop fusion | flops 42991616 | bytes 85983232 | tf_op jit(solution)/shard_map/add | solution.py:72
  116.6 6.3 %copy.12 = f32[512,2,8,128]{3,1,2,0:T(2,128)} copy(f32[512,2,8,128]{3,2,1,0:T(8,128)} %bitcast.43) | data formatting | bytes 8388608
  122.9 8.0 %scatter_fusion = f32[1048576]{0:T(1024)} fusion(f32[1048576]{0:T(1024)} %bitcast.40, s32[512]{0:T(512)S(1)} %bitcast.48, f32[512]{0:T(512)S(1)} %get-tuple-element.11), kind=kCustom, calls=%fused_computation.1 | custom fusion | flops 512 | bytes 8192 | tf_op jit(solution)/shard_map/scatter-add | solution.py:56
  130.9 1.7 fusion.49
  132.6 1.3 slice.244
  133.9 2.1 collective-permute-start.3
  136.0 0.3 slice.241
  136.3 2.3 collective-permute-start.2
  138.6 5.2 %reshape.178 = f32[16,256,256]{2,1,0:T(8,128)} reshape(f32[1048576]{0:T(1024)} %scatter_fusion) | data formatting | bytes 8388608 | tf_op jit(solution)/shard_map/reshape | solution.py:56
  143.7 15.5 %collective-permute-done.3 = f32[4,256,256]{2,1,0:T(8,128)S(1)} collective-permute-done((f32[4,256,256]{2,1,0:T(8,128)}, f32[4,256,256]{2,1,0:T(8,128)S(1)}, u32[]{:S(2)}, u32[]{:S(2)}) %collective-permute-start.3) | collective-permute-done | bytes 1048608 | tf_op jit(solution)/shard_map/ppermute | solution.py:18
  159.3 0.0 copy-start.2
  159.3 0.1 constant_dynamic-update-slice_fusion.3
  159.4 0.0 copy-start
  159.4 3.6 %constant_dynamic-update-slice_fusion.1 = (f32[20,256,256]{2,1,0:T(8,128)S(1)}, f32[20,256,256]{2,1,0:T(8,128)S(1)}) fusion(f32[16,256,256]{2,1,0:T(8,128)} %reshape.178, f32[20,256,256]{2,1,0:T(8,128)S(1)} %constant_dynamic-update-slice_fusion.3), kind=kLoop, calls=%fused_computation.101 | loop fusion | bytes 12582912
  163.0 0.0 copy-done.2
  163.0 0.0 copy-start.1
  163.0 0.0 collective-permute-done.2
  163.0 0.1 copy-done
  163.1 6.4 %select_maximum_fusion = f32[24,264,264]{2,1,0:T(8,128)S(1)} fusion(f32[4,256,256]{2,1,0:T(8,128)} %collective-permute-done.2, f32[16,256,256]{2,1,0:T(8,128)S(1)} %copy-done, f32[4,256,256]{2,1,0:T(8,128)} %copy-done.2), kind=kLoop, calls=%fused_computation.7 | loop fusion | flops 25090560 | bytes 12982272 | tf_op jit(solution)/shard_map/concatenate | solution.py:22
  169.6 1.3 constant_dynamic-update-slice_fusion
  170.9 0.0 copy-done.1
  170.9 20.0 %fusion.36 = f32[16,256,256]{2,1,0:T(8,128)} fusion(f32[16,256,256]{2,1,0:T(8,128)} %param.8, f32[24,264,264]{2,1,0:T(8,128)S(1)} %select_maximum_fusion, f32[20,256,256]{2,1,0:T(8,128)} %copy-done.1, f32[20,256,256]{2,1,0:T(8,128)S(1)} %constant_dynamic-update-slice_fusion, f32[16,256,256]{2,1,0:T(8,128)S(1)} %copy-done, f32[1,16,256,256]{3,2,1,0:T(8,128)} %param.7), kind=kLoop, calls=%fused_computation.60 | loop fusion | flops 34603008 | bytes 117440512 | tf_op jit(solution)/shard_map/add | solution.py:72
  190.9 6.3 %copy.14 = f32[512,2,8,128]{3,1,2,0:T(2,128)} copy(f32[512,2,8,128]{3,2,1,0:T(8,128)} %bitcast.42) | data formatting | bytes 8388608
  197.2 8.0 %scatter_fusion.1 = f32[1048576]{0:T(1024)} fusion(f32[1048576]{0:T(1024)} %bitcast.37, s32[512]{0:T(512)S(1)} %bitcast.49, f32[512]{0:T(512)S(1)} %get-tuple-element.10), kind=kCustom, calls=%fused_computation.2 | custom fusion | flops 512 | bytes 8192 | tf_op jit(solution)/shard_map/scatter-add | solution.py:56
  205.2 5.2 %reshape.180 = f32[16,256,256]{2,1,0:T(8,128)} reshape(f32[1048576]{0:T(1024)} %scatter_fusion.1) | data formatting | bytes 8388608 | tf_op jit(solution)/shard_map/reshape | solution.py:56
  210.4 18.9 %slice.269 = f32[8,128,128]{2,1,0:T(8,128)S(1)} slice(f32[16,256,256]{2,1,0:T(8,128)} %reshape.180), slice={[0:16:2], [0:256:2], [0:256:2]} | slice | bytes 1048576 | tf_op jit(solution)/shard_map/slice | solution.py:75
  229.2 1.1 copy.9
  230.3 7.0 %all-to-all-start = ((f32[1,8,128,128]{3,1,0,2:T(8,128)}), f32[1,8,128,128]{3,1,0,2:T(8,128)S(1)}, u32[]{:S(2)}, u32[]{:S(2)}) async-start(f32[1,8,128,128]{3,1,0,2:T(8,128)} %copy.9), calls=%async_computation | async-start | bytes 1048576 | tf_op jit(solution)/shard_map/all_to_all | solution.py:77
  237.3 0.0 copy-start.3
  237.3 5.2 %broadcast_in_dim_reshape.3 = f32[1,16,256,256]{3,2,1,0:T(8,128)} reshape(f32[1048576]{0:T(1024)} %scatter_fusion.1) | data formatting | bytes 8388608 | tf_op jit(solution)/shard_map/broadcast_in_dim;reshape | solution.py:79
  242.6 3.3 %all-to-all-done = f32[1,8,128,128]{3,1,0,2:T(8,128)S(1)} async-done(((f32[1,8,128,128]{3,1,0,2:T(8,128)}), f32[1,8,128,128]{3,1,0,2:T(8,128)S(1)}, u32[]{:S(2)}, u32[]{:S(2)}) %all-to-all-start) | async-done | bytes 524320 | tf_op jit(solution)/shard_map/all_to_all | solution.py:77
  245.9 0.1 add_log_fusion
  246.0 0.0 copy-done.3
  246.0 0.6 copy.11
  (6 shorter events, 0.1 us)
Async XLA Ops:
  3.3 33.4 %collective-permute-start = (f32[4,256,256]{2,1,0:T(8,128)}, f32[4,256,256]{2,1,0:T(8,128)S(1)}, u32[]{:S(2)}, u32[]{:S(2)}) collective-permute-start(f32[4,256,256]{2,1,0:T(8,128)} %get-tuple-element.8), channel_id=1, source_target_pairs={{1,0},{2,1},{3,2},{4,3},{5,4},{6,5},{7,6},{8,7},{9,8},{10,9},{11,1... | collective-permute-start | bytes 3145736 | tf_op jit(solution)/shard_map/ppermute | solution.py:21
  6.7 30.1 %collective-permute-start.1 = (f32[4,256,256]{2,1,0:T(8,128)S(1)}, f32[4,256,256]{2,1,0:T(8,128)S(1)}, u32[]{:S(2)}, u32[]{:S(2)}) collective-permute-start(f32[4,256,256]{2,1,0:T(8,128)S(1)} %get-tuple-element.9), channel_id=1, source_target_pairs={{0,1},{1,2},{2,3},{3,4},{4,5},{5,6},{6,7},{7,8},{8,9},{9,10},{10,1... | collective-permute-start | bytes 3145736 | tf_op jit(solution)/shard_map/ppermute | solution.py:18
  10.2 6.4 %copy-start.4 = (s32[1,512]{1,0:T(1,128)S(1)}, s32[1,512]{1,0:T(1,128)}, u32[]{:S(2)}) copy-start(s32[1,512]{1,0:T(1,128)} %param.10) | copy-start | bytes 6148
  10.2 26.5 %copy-start.5 = (f32[1,2,512]{2,1,0:T(2,128)S(1)}, f32[1,2,512]{2,1,0:T(2,128)}, u32[]{:S(2)}) copy-start(f32[1,2,512]{2,1,0:T(2,128)} %param.9) | copy-start | bytes 12292
  133.9 25.4 %collective-permute-start.3 = (f32[4,256,256]{2,1,0:T(8,128)}, f32[4,256,256]{2,1,0:T(8,128)S(1)}, u32[]{:S(2)}, u32[]{:S(2)}) collective-permute-start(f32[4,256,256]{2,1,0:T(8,128)} %slice.244), channel_id=1, source_target_pairs={{0,1},{1,2},{2,3},{3,4},{4,5},{5,6},{6,7},{7,8},{8,9},{9,10},{10,1... | collective-permute-start | bytes 3145736 | tf_op jit(solution)/shard_map/ppermute | solution.py:18
  136.3 26.7 %collective-permute-start.2 = (f32[4,256,256]{2,1,0:T(8,128)S(1)}, f32[4,256,256]{2,1,0:T(8,128)}, u32[]{:S(2)}, u32[]{:S(2)}) collective-permute-start(f32[4,256,256]{2,1,0:T(8,128)S(1)} %slice.241), channel_id=1, source_target_pairs={{1,0},{2,1},{3,2},{4,3},{5,4},{6,5},{7,6},{8,7},{9,8},{10,9},{11,1... | collective-permute-start | bytes 3145736 | tf_op jit(solution)/shard_map/ppermute | solution.py:21
  159.3 3.7 %copy-start.2 = (f32[4,256,256]{2,1,0:T(8,128)}, f32[4,256,256]{2,1,0:T(8,128)S(1)}, u32[]{:S(2)}) copy-start(f32[4,256,256]{2,1,0:T(8,128)S(1)} %collective-permute-done.3) | copy-start | bytes 3145732
  159.4 3.8 %copy-start = (f32[16,256,256]{2,1,0:T(8,128)S(1)}, f32[16,256,256]{2,1,0:T(8,128)}, u32[]{:S(2)}) copy-start(f32[16,256,256]{2,1,0:T(8,128)} %reshape.178) | copy-start | bytes 12582916
  163.0 7.9 %copy-start.1 = (f32[20,256,256]{2,1,0:T(8,128)}, f32[20,256,256]{2,1,0:T(8,128)S(1)}, u32[]{:S(2)}) copy-start(f32[20,256,256]{2,1,0:T(8,128)S(1)} %get-tuple-element.5) | copy-start | bytes 15728644
  230.3 15.5 %all-to-all-start = ((f32[1,8,128,128]{3,1,0,2:T(8,128)}), f32[1,8,128,128]{3,1,0,2:T(8,128)S(1)}, u32[]{:S(2)}, u32[]{:S(2)}) async-start(f32[1,8,128,128]{3,1,0,2:T(8,128)} %copy.9), calls=%async_computation | async-start | bytes 1048576 | tf_op jit(solution)/shard_map/all_to_all | solution.py:77
  237.3 8.7 %copy-start.3 = (f32[8,16,128]{2,1,0:T(8,128)S(1)}, f32[8,16,128]{2,1,0:T(8,128)}, u32[]{:S(2)}) copy-start(f32[8,16,128]{2,1,0:T(8,128)} %param.11) | copy-start | bytes 196612
where the time goes:
time: 249 us; the launch traced here: 247 us
  other arithmetic  123 us (49%)
  local copies, waits for them, and re-layouts  86.2 us (35%)
  waiting for transfers between devices  18.8 us (8%)
  starting transfers between devices  18.2 us (7%)
    add x2, other arithmetic, on_device(): nxt = 2.0 * curr - prev + coefficient * laplace(padded)  91.2 us
    unnamed x18, local copies, waits for them, and re-layouts  23.4 us
    gather x1, local copies, waits for them, and re-layouts, inject(): amount = jnp.where(valid, coef_planes.reshape(-1)[local] * record_now, 0.0)  20 us
    slice x1, local copies, waits for them, and re-layouts, on_device(): sample = curr[::DEC, ::DEC, ::DEC]  18.9 us
    scatter-add x2, other arithmetic, inject(): return nxt.reshape(-1).at[local].add(amount).reshape(nxt.shape)  16 us
    ppermute x2, waiting for transfers between devices, with_halo(): lax.ppermute(lax.slice_in_dim(block, block.shape[dim] - width, None, axis...  15.5 us
    concatenate x2, other arithmetic, with_halo(): block = jnp.concatenate([low, block, high], axis=dim)  15.2 us
    reshape x2, local copies, waits for them, and re-layouts, inject(): return nxt.reshape(-1).at[local].add(amount).reshape(nxt.shape)  10.4 us
  transfers between devices with their start and end apart: 5, of which 2 were waited for; matrix products, arithmetic and copies ran while one was open for 17% of the time, Pallas kernels for 0%

commit v1 on v0

v1 whole, which is shorter than its diff:
```python
import functools

import jax
import jax.numpy as jnp
from jax import lax
from jax.experimental import pallas as pl
from jax.experimental.pallas import tpu as pltpu
from jax.sharding import PartitionSpec as P

SCALE = 5040.0
TAPS = (8064.0, -1008.0, 128.0, -9.0)
CENTRE = 3.0 * -14350.0
PAD = 4
CHUNKS = 8
NT = (((1,), (1,)), ((), ()))


def dot(a, b):
    return jnp.dot(a, b, preferred_element_type=jnp.float32)


def dot_nt(a, b):
    return lax.dot_general(a, b, NT, preferred_element_type=jnp.float32)


def split2(v):
    high = v.astype(jnp.bfloat16)
    return high, (v - high.astype(jnp.float32)).astype(jnp.bfloat16)


def kernel(
    prev_hbm, curr_hbm, coef_hbm, rec_ref, idx_ref, image_ref,
    field_hbm, image_out,
    older, newer, coef, halo, mixed, band, amounts, terms, from_x, from_z,
    load_sem, store_sem, halo_send, halo_recv, x_send, x_recv, z_send, z_recv,
):
    depth, nx, ny = coef.shape
    rows = nx // CHUNKS
    slabs = lax.axis_size("space")
    group = lax.axis_index("group")
    slab = lax.axis_index("space")
    my_x, my_z = group // 2, lax.rem(group, 2)
    has_low, has_high = slab > 0, slab < slabs - 1

    loads = [
        pltpu.make_async_copy(curr_hbm.at[0], newer.at[pl.ds(PAD, depth)], load_sem.at[0]),
        pltpu.make_async_copy(coef_hbm, coef, load_sem.at[1]),
        pltpu.make_async_copy(prev_hbm.at[0], older.at[pl.ds(PAD, depth)], load_sem.at[2]),
    ]
    for load in loads:
        load.start()

    barrier = pltpu.get_barrier_semaphore()

    @pl.when(has_low)
    def _():
        pl.semaphore_signal(barrier, inc=1, device_id={"space": slab - 1})

    @pl.when(has_high)
    def _():
        pl.semaphore_signal(barrier, inc=1, device_id={"space": slab + 1})

    for hop in range(1, 4):
        pl.semaphore_signal(barrier, inc=1, device_id={"group": lax.rem(my_x + hop, 4) * 2 + my_z})
    pl.semaphore_signal(barrier, inc=1, device_id={"group": my_x * 2 + 1 - my_z})
    pl.semaphore_wait(barrier, 4 + has_low.astype(jnp.int32) + has_high.astype(jnp.int32))

    def chunk_of(i):
        return lax.rem(my_x + 1 + i // 2, 4) * 2 + lax.rem(my_z + 1 + i, 2)

    def rows_of(i):
        return pl.ds(pl.multiple_of(chunk_of(i) * rows, rows), rows)

    def to_low(step, i):
        source = curr_hbm.at[0, pl.ds(0, PAD), rows_of(i)] if step == 0 else older.at[pl.ds(PAD, PAD), rows_of(i)]
        return pltpu.make_async_remote_copy(
            source, halo.at[step, 1, :, rows_of(i)], halo_send.at[step, 0, i], halo_recv.at[step, 1, i],
            device_id={"space": slab - 1},
        )

    def to_high(step, i):
        source = (
            curr_hbm.at[0, pl.ds(depth - PAD, PAD), rows_of(i)] if step == 0 else older.at[pl.ds(depth, PAD), rows_of(i)]
        )
        return pltpu.make_async_remote_copy(
            source, halo.at[step, 0, :, rows_of(i)], halo_send.at[step, 1, i], halo_recv.at[step, 0, i],
            device_id={"space": slab + 1},
        )

    def send(step, i):
        @pl.when(has_low)
        def _():
            to_low(step, i).start()

        @pl.when(has_high)
        def _():
            to_high(step, i).start()

    @pl.loop(0, CHUNKS)
    def _(i):
        send(0, i)

    for ref in (older, newer):
        zero = jnp.zeros((PAD, nx, ny), jnp.float32)
        ref[pl.ds(0, PAD)] = zero
        ref[pl.ds(PAD + depth, PAD)] = zero
    apart = jnp.abs(
        lax.broadcasted_iota(jnp.int32, (nx, nx), 0) - lax.broadcasted_iota(jnp.int32, (nx, nx), 1)
    )
    matrix = jnp.zeros((nx, nx), jnp.float32)
    for j, tap in enumerate(TAPS):
        matrix = jnp.where(apart == j + 1, tap, matrix)
    band[...] = matrix.astype(jnp.bfloat16)
    index = idx_ref[...]
    receivers = index.shape[1]
    at_y = lax.broadcasted_iota(jnp.int32, (ny, receivers), 0) == (index & (ny - 1))
    for step in range(2):
        high, low = split2(rec_ref[0, pl.ds(step, 1), :] * SCALE)
        amounts[step, 0] = jnp.where(at_y, high.astype(jnp.float32), 0.0).astype(jnp.bfloat16)
        amounts[step, 1] = jnp.where(at_y, low.astype(jnp.float32), 0.0).astype(jnp.bfloat16)

    for load in loads:
        load.wait()

    def base(step, field, other):
        @pl.loop(0, depth)
        def _(z):
            high, low = split2(field[z + PAD])
            first = (slab * depth + z) * nx
            at_row = lax.broadcasted_iota(jnp.int32, (nx, receivers), 0) + first == (index >> 8)
            onehot = jnp.where(at_row, 1.0, 0.0).astype(jnp.bfloat16)
            mixed[...] = (
                dot(high, band[...]) + dot(low, band[...])
                + dot(band[...], high) + dot(band[...], low)
                + dot_nt(onehot, amounts[step, 0]) + dot_nt(onehot, amounts[step, 1])
            )

            @pl.loop(0, CHUNKS)
            def _(b):
                part = pl.ds(pl.multiple_of(b * rows, rows), rows)
                centre = field[z + PAD, part]
                total = CENTRE * centre + mixed[part]
                for j, tap in enumerate(TAPS):
                    total += tap * (field[z + PAD + j + 1, part] + field[z + PAD - j - 1, part])
                other[z + PAD, part] = 2.0 * centre - other[z + PAD, part] + (coef[z, part] * (1.0 / SCALE)) * total

    def add_halo(step, i, other):
        part = rows_of(i)

        @pl.when(has_low)
        def _():
            to_high(step, i).wait_recv()
            for k in range(PAD):
                total = TAPS[k] * halo[step, 0, PAD - 1, part]
                for j in range(k + 1, PAD):
                    total += TAPS[j] * halo[step, 0, PAD + k - j - 1, part]
                other[PAD + k, part] += (coef[k, part] * (1.0 / SCALE)) * total

        @pl.when(has_high)
        def _():
            to_low(step, i).wait_recv()
            for k in range(PAD):
                total = TAPS[k] * halo[step, 1, 0, part]
                for j in range(k + 1, PAD):
                    total += TAPS[j] * halo[step, 1, j - k, part]
                z = depth - 1 - k
                other[PAD + z, part] += (coef[z, part] * (1.0 / SCALE)) * total

    base(0, newer, older)

    @pl.loop(0, CHUNKS)
    def _(i):
        add_halo(0, i, older)
        send(1, i)

    base(1, older, newer)

    half = rows // 2
    planes = depth // 2
    even = jnp.where(
        lax.broadcasted_iota(jnp.int32, (ny // 2, ny), 1) == 2 * lax.broadcasted_iota(jnp.int32, (ny // 2, ny), 0), 1.0, 0.0
    ).astype(jnp.bfloat16)

    def store(i):
        return pltpu.make_async_copy(
            newer.at[pl.ds(PAD, depth), rows_of(i)], field_hbm.at[0, :, rows_of(i)], store_sem.at[i]
        )

    def term_of(i):
        add_halo(1, i, newer)
        store(i).start()
        part = rows_of(i)
        rest = jnp.concatenate([newer[PAD + 2 * p, part] for p in range(planes)], axis=0)
        sample = None
        for _ in range(3):
            piece = rest.astype(jnp.bfloat16)
            rest = rest - piece.astype(jnp.float32)
            picked = dot(even, dot_nt(piece, even).astype(jnp.bfloat16))
            sample = picked if sample is None else sample + picked
        return jnp.log(1.0 + sample * sample).reshape(planes, half, ny // 2)

    def to_x(i):
        other_x = chunk_of(i) // 2
        other_z = lax.rem(chunk_of(i), 2)
        return pltpu.make_async_remote_copy(
            terms.at[i], from_x.at[other_z, my_x], x_send.at[i], x_recv.at[other_z, my_x],
            device_id={"group": other_x * 2 + my_z},
        )

    @pl.loop(0, CHUNKS - 2)
    def _(i):
        terms[i] = term_of(i)
        to_x(i).start()

    def sum_x(total, which):
        for hop in range(1, 4):
            other_x = lax.rem(my_x + hop, 4)
            pltpu.make_async_remote_copy(
                terms.at[0], from_x.at[which, other_x], x_send.at[0], x_recv.at[which, other_x],
                device_id={"group": other_x * 2 + my_z},
            ).wait_recv()
            total += from_x[which, other_x]
        return total

    to_z = pltpu.make_async_remote_copy(
        terms.at[CHUNKS - 2], from_z, z_send, z_recv, device_id={"group": my_x * 2 + 1 - my_z}
    )
    terms[CHUNKS - 2] = sum_x(term_of(CHUNKS - 2), 1 - my_z)
    to_z.start()
    total = sum_x(term_of(CHUNKS - 1), my_z)
    to_z.wait_recv()
    total += from_z[...]
    image_out[...] = image_ref[...] + (jnp.exp(total * 0.125) - 1.0)

    to_z.wait_send()

    @pl.loop(0, CHUNKS - 2)
    def _(i):
        to_x(i).wait_send()

    @pl.loop(0, CHUNKS)
    def _(i):
        store(i).wait()
        for step in range(2):
            @pl.when(has_low)
            def _():
                to_low(step, i).wait_send()

            @pl.when(has_high)
            def _():
                to_high(step, i).wait_send()


def on_device(prev_field, curr_field, coefficient, recordings, receivers, image_in):
    depth, nx, ny = coefficient.shape
    _, steps, count = recordings.shape
    padded = (depth + 2 * PAD, nx, ny)
    image = image_in.shape
    anywhere = pl.BlockSpec(memory_space=pl.ANY)
    vmem = pl.BlockSpec(memory_space=pltpu.VMEM)
    dma = pltpu.SemaphoreType.DMA
    return pl.pallas_call(
        kernel,
        out_shape=(
            jax.ShapeDtypeStruct(curr_field.shape, jnp.float32),
            jax.ShapeDtypeStruct(image, jnp.float32),
        ),
        in_specs=[anywhere, anywhere, anywhere, vmem, vmem, vmem],
        out_specs=(anywhere, vmem),
        scratch_shapes=[
            pltpu.VMEM(padded, jnp.float32),
            pltpu.VMEM(padded, jnp.float32),
            pltpu.VMEM((depth, nx, ny), jnp.float32),
            pltpu.VMEM((steps, 2, PAD, nx, ny), jnp.float32),
            pltpu.VMEM((nx, ny), jnp.float32),
            pltpu.VMEM((nx, nx), jnp.bfloat16),
            pltpu.VMEM((steps, 2, ny, count), jnp.bfloat16),
            pltpu.VMEM((CHUNKS,) + image, jnp.float32),
            pltpu.VMEM((2, 4) + image, jnp.float32),
            pltpu.VMEM(image, jnp.float32),
            dma((3,)), dma((CHUNKS,)),
            dma((steps, 2, CHUNKS)), dma((steps, 2, CHUNKS)),
            dma((CHUNKS,)), dma((2, 4)), dma, dma,
        ],
        compiler_params=pltpu.CompilerParams(
            collective_id=0, has_side_effects=True, vmem_limit_bytes=56 * 1024 * 1024
        ),
    )(prev_field, curr_field, coefficient, recordings, receivers, image_in)


def solution(mesh):
    placed = (
        P("group", "space", None, None),
        P("group", "space", None, None),
        P("space", None, None),
        P("group", None, None),
        P("group", None),
        P("space", "group", None),
    )
    return jax.shard_map(
        on_device,
        mesh=mesh,
        in_specs=placed,
        out_specs=(P("group", "space", None, None), P("space", "group", None)),
        check_vma=False,
    )
```

time: 249 us -> 70.8 us (0.28)
  the two profiles are of different devices: /device:TPU:1 before, /device:TPU:27 now
where the time goes in v1:
time: 70.8 us; the launch traced here: 70.6 us
  Pallas kernels  64.7 us (91%)
  local copies, waits for them, and re-layouts  5.26 us (7%)
    pallas_call x1, Pallas kernels, on_device(): pl.pallas_call(kernel, out_shape=(jax.ShapeDtypeStruct(curr_field.shape,...  64.7 us
    unnamed x4, local copies, waits for them, and re-layouts  5.26 us

profile of v1, /device:TPU:27, one launch (start us, length us, event | category | flops | bytes accessed | tf_op | source)
XLA Modules:
  0.0 70.6 jit_solution(10301220828160696960)
XLA Ops:
  0.6 64.7 %shard_map.77 = (f32[1,16,256,256]{3,2,1,0:T(8,128)}, f32[8,16,128]{2,1,0:T(8,128)}) custom-call(f32[1,16,256,256]{3,2,1,0:T(8,128)} %prev_hbm.1, f32[1,16,256,256]{3,2,1,0:T(8,128)} %curr_hbm.1, f32[16,256,256]{2,1,0:T(8,128)} %coef_hbm.1, f32[1,2,512]{2,1,0:T(2,128)} %rec_ref.1, s32[1,512]{1,0:T(1,128)} %idx_ref.1, f32[8,16,128]{2,1,0:T(8,128)} %image_ref.1), custom_call_target="tpu_custom_call" | custom-call | tf_op jit(solution)/shard_map/pallas_call | solution.py:262
  65.4 0.0 copy-start
  65.4 4.6 %copy.10 = f32[1,16,256,256]{3,2,1,0:T(8,128)} copy(f32[1,16,256,256]{3,2,1,0:T(8,128)} %get-tuple-element.4) | data formatting | bytes 8388608
  70.0 0.0 copy-done
  70.0 0.6 copy.11
Async XLA Ops:
  65.4 4.6 %copy-start = (f32[8,16,128]{2,1,0:T(8,128)S(1)}, f32[8,16,128]{2,1,0:T(8,128)}, u32[]{:S(2)}) copy-start(f32[8,16,128]{2,1,0:T(8,128)} %get-tuple-element.5) | copy-start | bytes 196612

commit v2 on v0

v2 whole, which is shorter than its diff:
```python
import jax
import jax.numpy as jnp
from jax import lax
from jax.experimental import pallas as pl
from jax.experimental.pallas import tpu as pltpu
from jax.sharding import PartitionSpec as P

SCALE = 5040.0
TAPS = (8064.0, -1008.0, 128.0, -9.0)
CENTRE = 3.0 * -14350.0
PAD = 4
CHUNKS = 8
ROWS = 4
BLOCK = 32
NT = (((1,), (1,)), ((), ()))


def dot(a, b):
    return jnp.dot(a, b, preferred_element_type=jnp.float32)


def dot_nt(a, b):
    return lax.dot_general(a, b, NT, preferred_element_type=jnp.float32)


def split2(v):
    high = v.astype(jnp.bfloat16)
    return high, (v - high.astype(jnp.float32)).astype(jnp.bfloat16)


def iota(shape, dim):
    return lax.broadcasted_iota(jnp.int32, shape, dim)


def kernel(
    prev_hbm, curr_hbm, coef_hbm, rec_ref, idx_ref, image_ref,
    field, image_out,
    older, newer, coef, far, near, relay, mixed, band, amounts, early, late, from_x, from_z, from_late,
    load_sem, far_send, far_recv, near_send, near_recv, via_recv, pass_send,
    x_send, x_recv, z_send, z_recv, late_send, late_recv,
):
    depth, nx, ny = coef.shape
    rows = nx // CHUNKS
    slabs = lax.axis_size("space")
    group = lax.axis_index("group")
    slab = lax.axis_index("space")
    my_x, my_z = group // 2, lax.rem(group, 2)
    core = lax.rem(slab, 2)
    far_slab, near_slab = slab - 1 + 2 * core, slab + 1 - 2 * core
    has_far = (slab > 0) & (slab < slabs - 1)
    far_start, near_start = core * (depth - PAD), (1 - core) * (depth - PAD)

    row, place = slab // 4, lax.rem(slab, 4)
    corner = (place == 0) | (place == 3)
    turn = 1 - 2 * core
    by_relay = jnp.where(corner, core * (2 * ROWS - 2 - 2 * row) + (1 - core) * 2 * row, 0)
    relayed = jnp.where(corner, (1 - core) * (2 * ROWS - 2 - 2 * row) + core * 2 * row, 0)
    partner, onward, behind = slab + 3 * turn, slab + 4 * turn, slab - 4 * turn
    has_onward = corner & (onward >= 0) & (onward < slabs)
    has_behind = corner & (behind >= 0) & (behind < slabs)

    def plane(p):
        return p + core * (depth - 1 - 2 * p)

    loads = [
        pltpu.make_async_copy(curr_hbm.at[0], newer.at[pl.ds(PAD, depth)], load_sem.at[0]),
        pltpu.make_async_copy(coef_hbm, coef, load_sem.at[1]),
        pltpu.make_async_copy(prev_hbm.at[0], older.at[pl.ds(PAD, depth)], load_sem.at[2]),
    ]
    for load in loads:
        load.start()

    barrier = pltpu.get_barrier_semaphore()

    def greet(there, slab_id):
        @pl.when(there)
        def _():
            pl.semaphore_signal(barrier, inc=1, device_id={"space": slab_id})

    pl.semaphore_signal(barrier, inc=1, device_id={"space": near_slab})
    greet(has_far, far_slab)
    greet(corner, partner)
    greet(has_onward, onward)
    greet(has_behind, behind)
    for hop in range(1, 8):
        pl.semaphore_signal(barrier, inc=1, device_id={"group": lax.rem(group + hop, 8)})
    pl.semaphore_wait(barrier, 8 + sum(there.astype(jnp.int32) for there in (has_far, corner, has_onward, has_behind)))

    def chunk_of(i):
        return lax.rem(my_x + 1 + i, 4) * 2 + lax.rem(my_z + 1 + i // 4, 2)

    def rows_of(i):
        return pl.ds(pl.multiple_of(chunk_of(i) * rows, rows), rows)

    def face(step, i):
        if step == 0:
            return curr_hbm.at[0, pl.ds(far_start, PAD), rows_of(i)]
        return older.at[pl.ds(PAD + far_start, PAD), rows_of(i)]

    def far_copy(step, i):
        return pltpu.make_async_remote_copy(
            face(step, i), far.at[step, :, rows_of(i)], far_send.at[step, i], far_recv.at[step, i],
            device_id={"space": far_slab},
        )

    def via_copy(step, i):
        return pltpu.make_async_remote_copy(
            face(step, i), relay.at[step, :, rows_of(i)], far_send.at[step, i], via_recv.at[step, i],
            device_id={"space": partner},
        )

    def pass_copy(step, i):
        return pltpu.make_async_remote_copy(
            relay.at[step, :, rows_of(i)], far.at[step, :, rows_of(i)], pass_send.at[step, i], far_recv.at[step, i],
            device_id={"space": onward},
        )

    def send_far(step, i):
        @pl.when(i < by_relay)
        def _():
            via_copy(step, i).start()

        @pl.when(i >= by_relay)
        def _():
            far_copy(step, i).start()

    def pass_on(step):
        @pl.loop(0, relayed)
        def _(i):
            via_copy(step, i).wait_recv()
            pass_copy(step, i).start()

    def near_copy(step):
        source = curr_hbm.at[0, pl.ds(near_start, PAD)] if step == 0 else older.at[pl.ds(PAD + near_start, PAD)]
        return pltpu.make_async_remote_copy(
            source, near.at[step], near_send.at[step], near_recv.at[step], device_id={"space": near_slab}
        )

    @pl.when(has_far)
    def _():
        @pl.loop(0, CHUNKS)
        def _(i):
            send_far(0, i)

    near_copy(0).start()

    for ref in (older, newer):
        zero = jnp.zeros((PAD, nx, ny), jnp.float32)
        ref[pl.ds(0, PAD)] = zero
        ref[pl.ds(PAD + depth, PAD)] = zero
    apart = jnp.abs(iota((nx, nx), 0) - iota((nx, nx), 1))
    matrix = jnp.zeros((nx, nx), jnp.float32)
    for j, tap in enumerate(TAPS):
        matrix = jnp.where(apart == j + 1, tap, matrix)
    band[...] = matrix.astype(jnp.bfloat16)
    index = idx_ref[...]
    receivers = index.shape[1]
    at_y = iota((ny, receivers), 0) == (index & (ny - 1))
    for step in range(2):
        high, low = split2(rec_ref[0, pl.ds(step, 1), :] * SCALE)
        amounts[step, 0] = jnp.where(at_y, high.astype(jnp.float32), 0.0).astype(jnp.bfloat16)
        amounts[step, 1] = jnp.where(at_y, low.astype(jnp.float32), 0.0).astype(jnp.bfloat16)

    for load in loads:
        load.wait()

    def mix(step, field_ref, z):
        value = field_ref[pl.ds(z + PAD, PAD)].reshape(PAD * nx, ny)
        high, low = split2(value)
        along_y = dot(high, band[...]) + dot(low, band[...])
        beside = [jnp.concatenate([v[k * nx : (k + 1) * nx] for k in range(PAD)], axis=1) for v in (high, low)]
        along_x = dot(band[...], beside[0]) + dot(band[...], beside[1])
        at_row = iota((PAD * nx, receivers), 0) + (slab * depth + z) * nx == (index >> 8)
        onehot = jnp.where(at_row, 1.0, 0.0).astype(jnp.bfloat16)
        injected = dot_nt(onehot, amounts[step, 0]) + dot_nt(onehot, amounts[step, 1])
        for k in range(PAD):
            mixed[z + k] = (along_y + injected)[k * nx : (k + 1) * nx] + along_x[:, k * ny : (k + 1) * ny]

    def update(z, field_ref, old_ref, old_pad, new_ref, new_pad):
        @pl.loop(0, nx // BLOCK)
        def _(b):
            part = pl.ds(pl.multiple_of(b * BLOCK, BLOCK), BLOCK)
            window = [field_ref[z + k, part] for k in range(3 * PAD)]
            for k in range(PAD):
                centre = window[k + PAD]
                total = CENTRE * centre + mixed[z + k, part]
                for j, tap in enumerate(TAPS):
                    total += tap * (window[k + PAD + j + 1] + window[k + PAD - j - 1])
                new_ref[z + k + new_pad, part] = (
                    2.0 * centre - old_ref[z + k + old_pad, part] + (coef[z + k, part] * (1.0 / SCALE)) * total
                )

    quads = depth // PAD

    def quad(g):
        return pl.multiple_of((g + core * (quads - 1 - 2 * g)) * PAD, PAD)

    @pl.loop(0, quads)
    def _(g):
        mix(0, newer, g * PAD)
        update(g * PAD, newer, older, PAD, older, PAD)

    def add_halo(h, z_of, target, pad, part):
        for k in range(PAD):
            total = TAPS[k] * h(0, part)
            for j in range(k + 1, PAD):
                total += TAPS[j] * h(j - k, part)
            z = z_of(k)
            target[z + pad, part] += (coef[z, part] * (1.0 / SCALE)) * total

    def add_near(step, target, pad):
        near_copy(step).wait_recv()

        @pl.loop(0, nx // BLOCK)
        def _(b):
            add_halo(
                lambda k, part: near[step, k + core * (PAD - 1 - 2 * k), part],
                lambda k: plane(depth - 1 - k),
                target, pad, pl.ds(pl.multiple_of(b * BLOCK, BLOCK), BLOCK),
            )

    def add_far(step, i, target, pad):
        far_copy(step, i).wait_recv()
        add_halo(
            lambda k, part: far[step, (PAD - 1 - k) + core * (2 * k - PAD + 1), part],
            plane, target, pad, rows_of(i),
        )

    add_near(0, older, PAD)
    near_copy(1).start()
    pass_on(0)

    @pl.loop(1, quads)
    def _(g):
        mix(1, older, quad(g))

    @pl.loop(2, quads)
    def _(g):
        update(quad(g), older, newer, PAD, field.at[0], 0)

    @pl.when(has_far)
    def _():
        @pl.loop(0, CHUNKS)
        def _(i):
            add_far(0, i, older, PAD)
            send_far(1, i)

    mix(1, older, quad(0))

    @pl.loop(0, 2)
    def _(g):
        update(quad(g), older, newer, PAD, field.at[0], 0)

    add_near(1, field.at[0], 0)

    half = rows // 2
    even = jnp.where(iota((ny // 2, ny), 1) == 2 * iota((ny // 2, ny), 0), 1.0, 0.0).astype(jnp.bfloat16)

    def terms_of(planes):
        size = planes[0].shape[0]
        value = jnp.concatenate(planes, axis=0)
        pieces = []
        for _ in range(3):
            pieces.append(value.astype(jnp.bfloat16))
            value = value - pieces[-1].astype(jnp.float32)
        columns = dot_nt(jnp.concatenate(pieces, axis=0), even).astype(jnp.bfloat16)
        count = 3 * len(planes)
        columns = jnp.concatenate([columns[n * size : (n + 1) * size] for n in range(count)], axis=1)
        picked = dot(even[: size // 2, :size], columns)
        width = ny // 2
        result = []
        for k in range(len(planes)):
            one, two, three = (picked[:, (k + p * len(planes)) * width :][:, :width] for p in range(3))
            sample = one + two + three
            result.append(jnp.log(1.0 + sample * sample))
        return result

    count = PAD // 2
    first_early, first_late = (1 - core) * count, core * (depth // 2 - count)

    @pl.loop(0, depth // 2 - count, step=2)
    def _(q):
        for k, term in enumerate(terms_of([field[0, 2 * (first_early + q + k)] for k in range(2)])):
            early[:, q + k] = term.reshape(CHUNKS, half, ny // 2)

    def to_x(hop, which):
        other = lax.rem(my_x + hop, 4)
        return pltpu.make_async_remote_copy(
            early.at[other * 2 + which], from_x.at[which, hop - 1], x_send.at[which, hop - 1], x_recv.at[which, hop - 1],
            device_id={"group": other * 2 + my_z},
        )

    away, mine = my_x * 2 + 1 - my_z, group
    to_z = pltpu.make_async_remote_copy(early.at[away], from_z, z_send, z_recv, device_id={"group": away})

    @pl.loop(0, 6)
    def _(n):
        to_x(1 + n // 2, lax.rem(n, 2)).start()

    def sum_x(which):
        total = early[my_x * 2 + which]
        for hop in range(1, 4):
            to_x(hop, which).wait_recv()
            total += from_x[which, hop - 1]
        return total

    def late_terms(i):
        @pl.when(has_far)
        def _():
            add_far(1, i, field.at[0], 0)

        part = rows_of(i)
        return terms_of([field[0, 2 * (first_late + q), part] for q in range(count)])

    def to_owner(i):
        return pltpu.make_async_remote_copy(
            late.at[i], from_late.at[i], late_send.at[i], late_recv.at[i], device_id={"group": chunk_of(i)}
        )

    def late_chunk(i):
        for q, term in enumerate(late_terms(i)):
            late[i, q] = term
        to_owner(i).start()

    pass_on(1)

    @pl.loop(0, 4)
    def _(i):
        late_chunk(i)

    early[away] = sum_x(1 - my_z)
    to_z.start()
    early[mine] = sum_x(my_z)

    @pl.loop(4, CHUNKS - 1)
    def _(i):
        late_chunk(i)

    to_z.wait_recv()
    at_early = pl.ds(first_early, depth // 2 - count)
    image_out[at_early] = image_ref[at_early] + (jnp.exp((early[mine] + from_z[...]) * 0.125) - 1.0)
    last = late_terms(CHUNKS - 1)
    for i in range(CHUNKS - 1):
        to_owner(i).wait_recv()
    for q in range(count):
        total = last[q]
        for i in range(CHUNKS - 1):
            total += from_late[i, q]
        image_out[first_late + q] = image_ref[first_late + q] + (jnp.exp(total * 0.125) - 1.0)

    to_z.wait_send()
    for step in range(2):
        near_copy(step).wait_send()

    @pl.loop(0, 6)
    def _(n):
        to_x(1 + n // 2, lax.rem(n, 2)).wait_send()

    @pl.loop(0, CHUNKS - 1)
    def _(i):
        to_owner(i).wait_send()

    for step in range(2):
        @pl.loop(0, relayed)
        def _(i):
            pass_copy(step, i).wait_send()

    @pl.when(has_far)
    def _():
        @pl.loop(0, CHUNKS)
        def _(i):
            for step in range(2):
                far_copy(step, i).wait_send()


def write_out(field, image, field_hbm, image_hbm, sems):
    parts = sems.shape[0] - 1
    planes = field.shape[1] // parts
    copies = [
        pltpu.make_async_copy(field.at[:, pl.ds(i * planes, planes)], field_hbm.at[:, pl.ds(i * planes, planes)], sems.at[i])
        for i in range(parts)
    ]
    copies.append(pltpu.make_async_copy(image, image_hbm, sems.at[parts]))
    for copy in copies:
        copy.start()
    for copy in copies:
        copy.wait()


def on_device(prev_field, curr_field, coefficient, recordings, receivers, image_in):
    depth, nx, ny = coefficient.shape
    _, steps, count = recordings.shape
    padded = (depth + 2 * PAD, nx, ny)
    image = image_in.shape
    early, late = (image[0] - PAD // 2,) + image[1:], (PAD // 2,) + image[1:]
    anywhere = pl.BlockSpec(memory_space=pl.ANY)
    vmem = pl.BlockSpec(memory_space=pltpu.VMEM)
    dma = pltpu.SemaphoreType.DMA
    f32 = jnp.float32
    field, image_out = pl.pallas_call(
        kernel,
        out_shape=(pltpu.VMEM(curr_field.shape, f32), pltpu.VMEM(image, f32)),
        in_specs=[anywhere, anywhere, anywhere, vmem, vmem, vmem],
        out_specs=(vmem, vmem),
        scratch_shapes=[
            pltpu.VMEM(padded, f32),
            pltpu.VMEM(padded, f32),
            pltpu.VMEM((depth, nx, ny), f32),
            pltpu.VMEM((steps, PAD, nx, ny), f32),
            pltpu.VMEM((steps, PAD, nx, ny), f32),
            pltpu.VMEM((steps, PAD, nx, ny), f32),
            pltpu.VMEM((depth, nx, ny), f32),
            pltpu.VMEM((nx, nx), jnp.bfloat16),
            pltpu.VMEM((steps, 2, ny, count), jnp.bfloat16),
            pltpu.VMEM((CHUNKS,) + early, f32),
            pltpu.VMEM((CHUNKS - 1,) + late, f32),
            pltpu.VMEM((2, 3) + early, f32),
            pltpu.VMEM(early, f32),
            pltpu.VMEM((CHUNKS - 1,) + late, f32),
            dma((3,)), dma((steps, CHUNKS)), dma((steps, CHUNKS)), dma((steps,)), dma((steps,)),
            dma((steps, CHUNKS)), dma((steps, CHUNKS)),
            dma((2, 3)), dma((2, 3)), dma, dma, dma((CHUNKS - 1,)), dma((CHUNKS - 1,)),
        ],
        compiler_params=pltpu.CompilerParams(
            collective_id=0, has_side_effects=True, vmem_limit_bytes=59 * 1024 * 1024
        ),
    )(prev_field, curr_field, coefficient, recordings, receivers, image_in)
    return pl.pallas_call(
        write_out,
        out_shape=(jax.ShapeDtypeStruct(curr_field.shape, f32), jax.ShapeDtypeStruct(image, f32)),
        in_specs=[vmem, vmem],
        out_specs=(anywhere, anywhere),
        scratch_shapes=[dma((9,))],
        compiler_params=pltpu.CompilerParams(vmem_limit_bytes=1024 * 1024),
    )(pltpu.with_memory_space_constraint(field, pltpu.VMEM), pltpu.with_memory_space_constraint(image_out, pltpu.VMEM))


def solution(mesh):
    placed = (
        P("group", "space", None, None),
        P("group", "space", None, None),
        P("space", None, None),
        P("group", None, None),
        P("group", None),
        P("space", "group", None),
    )
    return jax.shard_map(
        on_device,
        mesh=mesh,
        in_specs=placed,
        out_specs=(P("group", "space", None, None), P("space", "group", None)),
        check_vma=False,
    )
```

time: 249 us -> 55.4 us (0.22)
  other arithmetic: 123 us -> 0 us
  local copies, waits for them, and re-layouts: 86.2 us -> 0 us
  Pallas kernels: 0 us -> 54.6 us
  waiting for transfers between devices: 18.8 us -> 0 us
  starting transfers between devices: 18.2 us -> 0 us
    add x3 -> x0, other arithmetic: 91.2 us -> none  [the longest x2 91.2 us: on_device(): nxt = 2.0 * curr - prev + coefficient * laplace(padded)]
    pallas_call x0 -> x2, Pallas kernels: none -> 54.6 us  [the longest x1 52.5 us: on_device(): pl.pallas_call(kernel, out_shape=(pltpu.VMEM(curr_field.shape, f32), pltp...]
    slice x6 -> x0, local copies, waits for them, and re-layouts: 24.8 us -> none  [the longest x1 18.9 us: on_device(): sample = curr[::DEC, ::DEC, ::DEC]]
    unnamed x18 -> x0, local copies, waits for them, and re-layouts: 23.4 us -> none
    gather x1 -> x0, local copies, waits for them, and re-layouts: 20 us -> none  [inject(): amount = jnp.where(valid, coef_planes.reshape(-1)[local] * record_now, 0.0)]
    scatter-add x2 -> x0, other arithmetic: 16 us -> none  [inject(): return nxt.reshape(-1).at[local].add(amount).reshape(nxt.shape)]
    ppermute x4 -> x0, waiting for transfers between devices: 15.5 us -> none  [the longest x2 15.5 us: with_halo(): lax.ppermute(lax.slice_in_dim(block, block.shape[dim] - width, None, axis...]
    concatenate x2 -> x0, other arithmetic: 15.2 us -> none  [with_halo(): block = jnp.concatenate([low, block, high], axis=dim)]
  transfers between devices with their start and end apart: 5 -> 0, of which waited for: 2 -> 0; matrix products, arithmetic and copies ran while one was open for 17% -> 0% of each run, Pallas kernels for 0% -> 0%
where the time goes in v2:
time: 55.4 us; the launch traced here: 55.3 us
  Pallas kernels  54.6 us (99%)
  between operations  0.64 us (1%)
    pallas_call x1, Pallas kernels, on_device(): pl.pallas_call(kernel, out_shape=(pltpu.VMEM(curr_field.shape, f32), pltp...  52.5 us
    pallas_call x1, Pallas kernels, on_device(): pl.pallas_call(write_out, out_shape=(jax.ShapeDtypeStruct(curr_field.shap...  2.09 us

profile of v2, /device:TPU:1, one launch (start us, length us, event | category | flops | bytes accessed | tf_op | source)
XLA Modules:
  0.0 55.3 jit_solution(11524891975286713574)
XLA Ops:
  0.6 52.5 %shard_map.77 = (f32[1,16,256,256]{3,2,1,0:T(8,128)S(1)}, f32[8,16,128]{2,1,0:T(8,128)S(1)}) custom-call(f32[1,16,256,256]{3,2,1,0:T(8,128)} %prev_hbm.1, f32[1,16,256,256]{3,2,1,0:T(8,128)} %curr_hbm.1, f32[16,256,256]{2,1,0:T(8,128)} %coef_hbm.1, f32[1,2,512]{2,1,0:T(2,128)} %rec_ref.1, s32[1,512]{1,0:T(1,128)} %idx_ref.1, f32[8,16,128]{2,1,0:T(8,128)} %image_ref.1), custom_call_target="tpu_custom_call" | custom-call | tf_op jit(solution)/shard_map/pallas_call | solution.py:400
  53.2 2.1 %shard_map.78 = (f32[1,16,256,256]{3,2,1,0:T(8,128)}, f32[8,16,128]{2,1,0:T(8,128)}) custom-call(f32[1,16,256,256]{3,2,1,0:T(8,128)S(1)} %get-tuple-element.4.field, f32[8,16,128]{2,1,0:T(8,128)S(1)} %get-tuple-element.5.image), custom_call_target="tpu_custom_call" | custom-call | tf_op jit(solution)/shard_map/pallas_call | solution.py:428

commit v3 on v2

--- a/solution.py
+++ b/solution.py
@@ -35,9 +35,9 @@
 def kernel(
     prev_hbm, curr_hbm, coef_hbm, rec_ref, idx_ref, image_ref,
     field, image_out,
-    older, newer, coef, far, near, relay, mixed, band, amounts, early, late, from_x, from_z, from_late,
+    older, newer, coef, far, near, relay, mixed, band, amounts, early, late, from_x, from_z, from_late, away_late, from_late_z,
     load_sem, far_send, far_recv, near_send, near_recv, via_recv, pass_send,
-    x_send, x_recv, z_send, z_recv, late_send, late_recv,
+    x_send, x_recv, z_send, z_recv, late_send, late_recv, late_z_send, late_z_recv,
 ):
     depth, nx, ny = coef.shape
     rows = nx // CHUNKS
@@ -77,14 +77,15 @@
         def _():
             pl.semaphore_signal(barrier, inc=1, device_id={"space": slab_id})
 
-    pl.semaphore_signal(barrier, inc=1, device_id={"space": near_slab})
-    greet(has_far, far_slab)
+    pl.semaphore_signal(barrier, inc=1, device_id={"group": my_x * 2 + 1 - my_z})
+    for hop in (2, 1, 3):
+        pl.semaphore_signal(barrier, inc=1, device_id={"group": lax.rem(my_x + hop, 4) * 2 + my_z})
     greet(corner, partner)
     greet(has_onward, onward)
     greet(has_behind, behind)
-    for hop in range(1, 8):
-        pl.semaphore_signal(barrier, inc=1, device_id={"group": lax.rem(group + hop, 8)})
-    pl.semaphore_wait(barrier, 8 + sum(there.astype(jnp.int32) for there in (has_far, corner, has_onward, has_behind)))
+    greet(has_far, far_slab)
+    pl.semaphore_signal(barrier, inc=1, device_id={"space": near_slab})
+    pl.semaphore_wait(barrier, 5 + sum(there.astype(jnp.int32) for there in (has_far, corner, has_onward, has_behind)))
 
     def chunk_of(i):
         return lax.rem(my_x + 1 + i, 4) * 2 + lax.rem(my_z + 1 + i // 4, 2)
@@ -115,20 +116,27 @@
             device_id={"space": onward},
         )
 
-    def send_far(step, i):
-        @pl.when(i < by_relay)
-        def _():
-            via_copy(step, i).start()
-
-        @pl.when(i >= by_relay)
-        def _():
-            far_copy(step, i).start()
-
-    def pass_on(step):
-        @pl.loop(0, relayed)
-        def _(i):
-            via_copy(step, i).wait_recv()
-            pass_copy(step, i).start()
+    def order(m):
+        return lax.rem(m + core * (CHUNKS - by_relay), CHUNKS)
+
+    def partner_order(m):
+        return lax.rem(m + (1 - core) * (CHUNKS - relayed), CHUNKS)
+
+    def send_far(step, m):
+        @pl.when(m < by_relay)
+        def _():
+            via_copy(step, order(m)).start()
+
+        @pl.when(m >= by_relay)
+        def _():
+            far_copy(step, order(m)).start()
+
+    def pass_on(step, first, count):
+        for m in range(count):
+            @pl.when(first + m < relayed)
+            def _():
+                via_copy(step, partner_order(first + m)).wait_recv()
+                pass_copy(step, partner_order(first + m)).start()
 
     def near_copy(step):
         source = curr_hbm.at[0, pl.ds(near_start, PAD)] if step == 0 else older.at[pl.ds(PAD + near_start, PAD)]
@@ -228,11 +236,11 @@
 
     add_near(0, older, PAD)
     near_copy(1).start()
-    pass_on(0)
 
     @pl.loop(1, quads)
     def _(g):
         mix(1, older, quad(g))
+        pass_on(0, 2 * g - 2, 2)
 
     @pl.loop(2, quads)
     def _(g):
@@ -242,7 +250,7 @@
     def _():
         @pl.loop(0, CHUNKS)
         def _(i):
-            add_far(0, i, older, PAD)
+            add_far(0, order(i), older, PAD)
             send_far(1, i)
 
     mix(1, older, quad(0))
@@ -314,17 +322,21 @@
 
     def to_owner(i):
         return pltpu.make_async_remote_copy(
-            late.at[i], from_late.at[i], late_send.at[i], late_recv.at[i], device_id={"group": chunk_of(i)}
+            late.at[i], from_late.at[i], late_send.at[i], late_recv.at[i],
+            device_id={"group": lax.rem(my_x + 1 + i, 4) * 2 + my_z},
         )
 
     def late_chunk(i):
         for q, term in enumerate(late_terms(i)):
             late[i, q] = term
-        to_owner(i).start()
-
-    pass_on(1)
-
-    @pl.loop(0, 4)
+
+        @pl.when(i != 3)
+        def _():
+            to_owner(i).start()
+
+    pass_on(1, 0, 2 * ROWS - 2)
+
+    @pl.loop(0, 2)
     def _(i):
         late_chunk(i)
 
@@ -332,7 +344,19 @@
     to_z.start()
     early[mine] = sum_x(my_z)
 
-    @pl.loop(4, CHUNKS - 1)
+    @pl.loop(2, 5)
+    def _(i):
+        late_chunk(i)
+
+    late_to_z = pltpu.make_async_remote_copy(
+        away_late, from_late_z, late_z_send, late_z_recv, device_id={"group": away}
+    )
+    for i in range(3):
+        to_owner(i).wait_recv()
+    away_late[...] = late[3] + (from_late[0] + from_late[1] + from_late[2])
+    late_to_z.start()
+
+    @pl.loop(5, CHUNKS - 1)
     def _(i):
         late_chunk(i)
 
@@ -340,14 +364,14 @@
     at_early = pl.ds(first_early, depth // 2 - count)
     image_out[at_early] = image_ref[at_early] + (jnp.exp((early[mine] + from_z[...]) * 0.125) - 1.0)
     last = late_terms(CHUNKS - 1)
-    for i in range(CHUNKS - 1):
+    for i in range(4, CHUNKS - 1):
         to_owner(i).wait_recv()
+    late_to_z.wait_recv()
     for q in range(count):
-        total = last[q]
-        for i in range(CHUNKS - 1):
-            total += from_late[i, q]
+        total = last[q] + (from_late[4, q] + from_late[5, q]) + (from_late[6, q] + from_late_z[q])
         image_out[first_late + q] = image_ref[first_late + q] + (jnp.exp(total * 0.125) - 1.0)
 
+    late_to_z.wait_send()
     to_z.wait_send()
     for step in range(2):
         near_copy(step).wait_send()
@@ -358,12 +382,14 @@
 
     @pl.loop(0, CHUNKS - 1)
     def _(i):
-        to_owner(i).wait_send()
+        @pl.when(i != 3)
+        def _():
+            to_owner(i).wait_send()
 
     for step in range(2):
         @pl.loop(0, relayed)
         def _(i):
-            pass_copy(step, i).wait_send()
+            pass_copy(step, partner_order(i)).wait_send()
 
     @pl.when(has_far)
     def _():
@@ -417,9 +443,11 @@
             pltpu.VMEM((2, 3) + early, f32),
             pltpu.VMEM(early, f32),
             pltpu.VMEM((CHUNKS - 1,) + late, f32),
+            pltpu.VMEM(late, f32),
+            pltpu.VMEM(late, f32),
             dma((3,)), dma((steps, CHUNKS)), dma((steps, CHUNKS)), dma((steps,)), dma((steps,)),
             dma((steps, CHUNKS)), dma((steps, CHUNKS)),
-            dma((2, 3)), dma((2, 3)), dma, dma, dma((CHUNKS - 1,)), dma((CHUNKS - 1,)),
+            dma((2, 3)), dma((2, 3)), dma, dma, dma((CHUNKS - 1,)), dma((CHUNKS - 1,)), dma, dma,
         ],
         compiler_params=pltpu.CompilerParams(
             collective_id=0, has_side_effects=True, vmem_limit_bytes=59 * 1024 * 1024

time: 55.4 us -> 54.3 us (0.980)
  Pallas kernels: 54.6 us -> 53.2 us
    pallas_call x1, Pallas kernels: 52.5 us -> 51.1 us  [on_device(): pl.pallas_call(kernel, out_shape=(pltpu.VMEM(curr_field.shape, f32), pltp...]
where the time goes in v3:
time: 54.3 us; the launch traced here: 53.9 us
  Pallas kernels  53.2 us (98%)
  between operations  0.64 us (1%)
    pallas_call x1, Pallas kernels, on_device(): pl.pallas_call(kernel, out_shape=(pltpu.VMEM(curr_field.shape, f32), pltp...  51.1 us
    pallas_call x1, Pallas kernels, on_device(): pl.pallas_call(write_out, out_shape=(jax.ShapeDtypeStruct(curr_field.shap...  2.09 us

profile of v3, /device:TPU:1, one launch (start us, length us, event | category | flops | bytes accessed | tf_op | source)
XLA Modules:
  0.0 53.9 jit_solution(13171469264411176889)
XLA Ops:
  0.6 51.1 %shard_map.77 = (f32[1,16,256,256]{3,2,1,0:T(8,128)S(1)}, f32[8,16,128]{2,1,0:T(8,128)S(1)}) custom-call(f32[1,16,256,256]{3,2,1,0:T(8,128)} %prev_hbm.1, f32[1,16,256,256]{3,2,1,0:T(8,128)} %curr_hbm.1, f32[16,256,256]{2,1,0:T(8,128)} %coef_hbm.1, f32[1,2,512]{2,1,0:T(2,128)} %rec_ref.1, s32[1,512]{1,0:T(1,128)} %idx_ref.1, f32[8,16,128]{2,1,0:T(8,128)} %image_ref.1), custom_call_target="tpu_custom_call" | custom-call | tf_op jit(solution)/shard_map/pallas_call | solution.py:426
  51.8 2.1 %shard_map.78 = (f32[1,16,256,256]{3,2,1,0:T(8,128)}, f32[8,16,128]{2,1,0:T(8,128)}) custom-call(f32[1,16,256,256]{3,2,1,0:T(8,128)S(1)} %get-tuple-element.4.field, f32[8,16,128]{2,1,0:T(8,128)S(1)} %get-tuple-element.5.image), custom_call_target="tpu_custom_call" | custom-call | tf_op jit(solution)/shard_map/pallas_call | solution.py:456

commit v4 on v3

--- a/solution.py
+++ b/solution.py
@@ -334,23 +334,29 @@
         def _():
             to_owner(i).start()
 
-    pass_on(1, 0, 2 * ROWS - 2)
+        @pl.when(jnp.logical_not(has_far))
+        def _():
+            pass_on(1, i, 1)
+
+    @pl.when(has_far)
+    def _():
+        pass_on(1, 0, 2 * ROWS - 2)
 
     @pl.loop(0, 2)
     def _(i):
         late_chunk(i)
 
+    @pl.loop(2, 5)
+    def _(i):
+        late_chunk(i)
+
+    late_to_z = pltpu.make_async_remote_copy(
+        away_late, from_late_z, late_z_send, late_z_recv, device_id={"group": away}
+    )
     early[away] = sum_x(1 - my_z)
     to_z.start()
     early[mine] = sum_x(my_z)
 
-    @pl.loop(2, 5)
-    def _(i):
-        late_chunk(i)
-
-    late_to_z = pltpu.make_async_remote_copy(
-        away_late, from_late_z, late_z_send, late_z_recv, device_id={"group": away}
-    )
     for i in range(3):
         to_owner(i).wait_recv()
     away_late[...] = late[3] + (from_late[0] + from_late[1] + from_late[2])

time: 54.3 us -> 54.2 us (level)
  no operation moved by 1% of the time
where the time goes in v4:
time: 54.2 us; the launch traced here: 54 us
  Pallas kernels  53.4 us (99%)
  between operations  0.64 us (1%)
    pallas_call x1, Pallas kernels, on_device(): pl.pallas_call(kernel, out_shape=(pltpu.VMEM(curr_field.shape, f32), pltp...  51.3 us
    pallas_call x1, Pallas kernels, on_device(): pl.pallas_call(write_out, out_shape=(jax.ShapeDtypeStruct(curr_field.shap...  2.09 us

profile of v4, /device:TPU:1, one launch (start us, length us, event | category | flops | bytes accessed | tf_op | source)
XLA Modules:
  0.0 54.0 jit_solution(17602852919324622693)
XLA Ops:
  0.6 51.3 %shard_map.77 = (f32[1,16,256,256]{3,2,1,0:T(8,128)S(1)}, f32[8,16,128]{2,1,0:T(8,128)S(1)}) custom-call(f32[1,16,256,256]{3,2,1,0:T(8,128)} %prev_hbm.1, f32[1,16,256,256]{3,2,1,0:T(8,128)} %curr_hbm.1, f32[16,256,256]{2,1,0:T(8,128)} %coef_hbm.1, f32[1,2,512]{2,1,0:T(2,128)} %rec_ref.1, s32[1,512]{1,0:T(1,128)} %idx_ref.1, f32[8,16,128]{2,1,0:T(8,128)} %image_ref.1), custom_call_target="tpu_custom_call" | custom-call | tf_op jit(solution)/shard_map/pallas_call | solution.py:432
  51.9 2.1 %shard_map.78 = (f32[1,16,256,256]{3,2,1,0:T(8,128)}, f32[8,16,128]{2,1,0:T(8,128)}) custom-call(f32[1,16,256,256]{3,2,1,0:T(8,128)S(1)} %get-tuple-element.4.field, f32[8,16,128]{2,1,0:T(8,128)S(1)} %get-tuple-element.5.image), custom_call_target="tpu_custom_call" | custom-call | tf_op jit(solution)/shard_map/pallas_call | solution.py:462

commit v5 on v4

--- a/solution.py
+++ b/solution.py
@@ -67,8 +67,6 @@
         pltpu.make_async_copy(coef_hbm, coef, load_sem.at[1]),
         pltpu.make_async_copy(prev_hbm.at[0], older.at[pl.ds(PAD, depth)], load_sem.at[2]),
     ]
-    for load in loads:
-        load.start()
 
     barrier = pltpu.get_barrier_semaphore()
 
@@ -151,6 +149,8 @@
             send_far(0, i)
 
     near_copy(0).start()
+    for load in loads:
+        load.start()
 
     for ref in (older, newer):
         zero = jnp.zeros((PAD, nx, ny), jnp.float32)
@@ -303,7 +303,7 @@
 
     @pl.loop(0, 6)
     def _(n):
-        to_x(1 + n // 2, lax.rem(n, 2)).start()
+        to_x(1 + lax.rem(n, 3), lax.rem(1 - my_z + n // 3, 2)).start()
 
     def sum_x(which):
         total = early[my_x * 2 + which]

time: 54.2 us -> 54.2 us (level)
  no operation moved by 1% of the time
where the time goes in v5:
time: 54.2 us; the launch traced here: 54 us
  Pallas kernels  53.4 us (99%)
  between operations  0.64 us (1%)
    pallas_call x1, Pallas kernels, on_device(): pl.pallas_call(kernel, out_shape=(pltpu.VMEM(curr_field.shape, f32), pltp...  51.3 us
    pallas_call x1, Pallas kernels, on_device(): pl.pallas_call(write_out, out_shape=(jax.ShapeDtypeStruct(curr_field.shap...  2.09 us

profile of v5, /device:TPU:1, one launch (start us, length us, event | category | flops | bytes accessed | tf_op | source)
XLA Modules:
  0.0 54.0 jit_solution(9553210090669866275)
XLA Ops:
  0.6 51.3 %shard_map.77 = (f32[1,16,256,256]{3,2,1,0:T(8,128)S(1)}, f32[8,16,128]{2,1,0:T(8,128)S(1)}) custom-call(f32[1,16,256,256]{3,2,1,0:T(8,128)} %prev_hbm.1, f32[1,16,256,256]{3,2,1,0:T(8,128)} %curr_hbm.1, f32[16,256,256]{2,1,0:T(8,128)} %coef_hbm.1, f32[1,2,512]{2,1,0:T(2,128)} %rec_ref.1, s32[1,512]{1,0:T(1,128)} %idx_ref.1, f32[8,16,128]{2,1,0:T(8,128)} %image_ref.1), custom_call_target="tpu_custom_call" | custom-call | tf_op jit(solution)/shard_map/pallas_call | solution.py:432
  51.9 2.1 %shard_map.78 = (f32[1,16,256,256]{3,2,1,0:T(8,128)}, f32[8,16,128]{2,1,0:T(8,128)}) custom-call(f32[1,16,256,256]{3,2,1,0:T(8,128)S(1)} %get-tuple-element.4.field, f32[8,16,128]{2,1,0:T(8,128)S(1)} %get-tuple-element.5.image), custom_call_target="tpu_custom_call" | custom-call | tf_op jit(solution)/shard_map/pallas_call | solution.py:462
